TPU v7x, 128 devices: a whole 4x4x4 slice. The times are simulated.
128 devices in a mesh: row: 16 (over y, x), col: 8 (over z, core).
Axes of the slice: x: 4, y: 4, z: 4, core: 2. Of those that a mesh axis runs over, the one named last changes fastest.
Arguments:
- cotangent: bfloat16 [49152, 256], P(('row', 'col')), may hold values from -6 to 6
- seed_label: int32 [49152], P(('row', 'col')), may hold values from 0 to 511
- tile_values: bfloat16 [16, 8, 16, 24, 128, 128], P('row', 'col'), may hold values from 0 to 0.008239746
- tile_rows: int32 [16, 8, 16, 24], P('row', 'col'), may hold values from 0 to 23
- tile_cols: int32 [16, 8, 16, 24], P('row', 'col'), may hold values from 0 to 2
- tile_scale: int32 [16, 8, 16, 24], P('row', 'col'), may hold values from 0 to 4
Outputs:
- first_grad: bfloat16 [49152, 256], P(('row', 'col'))
- label_grad: bfloat16 [49152, 256], P(('row', 'col'))
All inputs are finite; a program needn't handle non-finite values.
Results may differ from a plain program's by a relative error of at most 0.019.
Values may be sent and summed in bfloat16 or wider, within the bound.
A program may use at most 64 MiB of HBM per device.

v0:
```python
import jax
import jax.numpy as jnp
from jax import lax
from jax.sharding import PartitionSpec as P

ALPHA = 0.9


def group_term(sources, blocks, tile_item):
    tile_block, row_ids, col_ids, scale_ids = tile_item
    picked = jnp.take(sources, row_ids, axis=0)
    products = jnp.einsum("tij,tic->tjc", tile_block, picked, preferred_element_type=jnp.float32)
    weights = scale_ids.astype(jnp.float32)[:, None] * (
        col_ids[:, None] == jnp.arange(blocks, dtype=jnp.int32)[None, :]
    ).astype(jnp.float32)
    summed = jnp.einsum("tb,tjc->bjc", weights, products, precision=lax.Precision.HIGHEST)
    return summed.reshape(blocks * summed.shape[1], summed.shape[2])


def propagate(labels, tile_set, blocks):
    segment, classes = labels.shape
    tile_size = tile_set[0].shape[-1]
    gathered = lax.all_gather(labels, "col", axis=0, tiled=True)
    sources = gathered.reshape(gathered.shape[0] // tile_size, tile_size, classes)
    group_terms = lax.map(lambda tile_item: group_term(sources, blocks, tile_item), tile_set)
    flat_terms = group_terms.reshape(group_terms.shape[0] * segment, classes)
    return lax.psum_scatter(
        flat_terms.astype(jnp.bfloat16), "row", scatter_dimension=0, tiled=True
    ).astype(jnp.float32)


def local(cotangent, seed_label, tile_values, tile_rows, tile_cols, tile_scale):
    segment, classes = cotangent.shape
    blocks = segment // tile_values.shape[-1]
    tile_set = (tile_values[0, 0], tile_rows[0, 0], tile_cols[0, 0], tile_scale[0, 0])
    keep_mask = (seed_label[:, None] != jnp.arange(classes, dtype=jnp.int32)[None, :]).astype(
        jnp.float32
    )
    first_in = (cotangent.astype(jnp.float32) * keep_mask).astype(jnp.bfloat16)
    first_grad = (ALPHA * propagate(first_in, tile_set, blocks)).astype(jnp.bfloat16)
    second_in = (first_grad.astype(jnp.float32) * keep_mask).astype(jnp.bfloat16)
    second = propagate(second_in, tile_set, blocks)
    label_grad = ALPHA * second + (1.0 - ALPHA) * keep_mask * (
        cotangent.astype(jnp.float32) + first_grad.astype(jnp.float32)
    )
    return (first_grad, label_grad.astype(jnp.bfloat16))


def solution(mesh):
    return jax.shard_map(
        local,
        mesh=mesh,
        in_specs=(
            P(("row", "col"), None),
            P(("row", "col")),
            P("row", "col", None, None, None, None),
            P("row", "col", None, None),
            P("row", "col", None, None),
            P("row", "col", None, None),
        ),
        out_specs=(P(("row", "col"), None), P(("row", "col"), None)),
        check_vma=False,
    )
```

profile of v0, /device:TPU:1, one launch (start us, length us, event | category | flops | bytes accessed | tf_op | source)
XLA Modules:
  0.0 485.8 jit_solution(12221701026368019652)
XLA Ops:
  9.0 29.5 %all-gather.3.cloned.1.call-done = bf16[3072,256]{1,0:T(8,128)(2,1)} async-done(((bf16[384,256]{1,0:T(8,128)(2,1)}), bf16[3072,256]{1,0:T(8,128)(2,1)}) %all-gather.3.cloned.1.call-update) | async-done | bytes 1572880 | tf_op jit(solution)/shard_map/all_gather | solution.py:23
  38.5 2.0 broadcast.31.clone
  40.4 129.7 %while.20 = (s32[]{:T(128)}, bf16[16,384,256]{2,1,0:T(8,128)(2,1)}, s32[16,24]{1,0:T(8,128)}, s32[16,24]{1,0:T(8,128)}, bf16[16,24,128,128]{3,2,1,0:T(8,128)(2,1...) while((s32[]{:T(128)}, bf16[16,384,256]{2,1,0:T(8,128)(2,1)}, s32[16,24]{1,0:T(8,128)}, ...), condition=%wide.region_1.3_spmd, body=%wide.region_0.2_spmd.sunk | while | flops 230425904 | bytes 12785741 | solution.py:25
  41.8 1.8 fusion.63
  44.3 3.5 fusion.65
  49.9 1.8 fusion.63
  52.4 3.5 fusion.65
  58.0 1.8 fusion.63
  60.5 3.5 fusion.65
  66.1 1.8 fusion.63
  68.6 3.5 fusion.65
  76.7 3.5 fusion.65
  82.3 1.8 fusion.63
  84.8 3.5 fusion.65
  90.4 1.8 fusion.63
  92.9 3.5 fusion.65
  98.5 1.8 fusion.63
  101.0 3.5 fusion.65
  106.6 1.8 fusion.63
  109.1 3.5 fusion.65
  114.7 1.8 fusion.63
  117.2 3.5 fusion.65
  122.9 1.8 fusion.63
  125.4 3.5 fusion.65
  131.0 1.8 fusion.63
  133.5 3.5 fusion.65
  139.1 1.8 fusion.63
  141.6 3.5 fusion.65
  149.7 3.5 fusion.65
  155.3 1.8 fusion.63
  157.8 3.5 fusion.65
  165.9 3.5 fusion.65
  170.2 73.7 %reduce-scatter.3.cloned.1.call-done = bf16[384,256]{1,0:T(8,128)(2,1)} async-done(((bf16[6144,256]{1,0:T(8,128)(2,1)}), bf16[384,256]{1,0:T(8,128)(2,1)}) %reduce-scatter.3.cloned.1.call-update) | async-done | bytes 196624 | tf_op jit(solution)/shard_map/reduce_scatter | solution.py:27
  245.7 26.4 %all-gather.5.cloned.1.call-done = bf16[3072,256]{1,0:T(8,128)(2,1)} async-done(((bf16[384,256]{1,0:T(8,128)(2,1)}), bf16[3072,256]{1,0:T(8,128)(2,1)}) %all-gather.5.cloned.1.call-update) | async-done | bytes 1572880 | tf_op jit(solution)/shard_map/all_gather | solution.py:23
  272.1 2.0 broadcast.31
  274.1 129.7 %while.21 = (s32[]{:T(128)}, bf16[16,384,256]{2,1,0:T(8,128)(2,1)}, s32[16,24]{1,0:T(8,128)}, s32[16,24]{1,0:T(8,128)}, bf16[16,24,128,128]{3,2,1,0:T(8,128)(2,1...) while((s32[]{:T(128)}, bf16[16,384,256]{2,1,0:T(8,128)(2,1)}, s32[16,24]{1,0:T(8,128)}, ...), condition=%wide.region_4.6_spmd, body=%wide.region_3.5_spmd.sunk | while | flops 230425904 | bytes 12785741 | solution.py:25
  275.4 1.8 fusion.70
  278.0 3.5 fusion.72
  286.1 3.5 fusion.72
  291.7 1.8 fusion.70
  294.2 3.5 fusion.72
  299.8 1.8 fusion.70
  302.3 3.5 fusion.72
  307.9 1.8 fusion.70
  310.4 3.5 fusion.72
  316.0 1.8 fusion.70
  318.5 3.5 fusion.72
  326.6 3.5 fusion.72
  332.2 1.8 fusion.70
  334.7 3.5 fusion.72
  340.3 1.8 fusion.70
  342.8 3.5 fusion.72
  348.4 1.8 fusion.70
  350.9 3.5 fusion.72
  356.5 1.8 fusion.70
  359.0 3.5 fusion.72
  364.6 1.8 fusion.70
  367.1 3.5 fusion.72
  372.7 1.8 fusion.70
  375.2 3.5 fusion.72
  383.3 3.5 fusion.72
  391.5 3.5 fusion.72
  399.6 3.5 fusion.72
  403.8 73.7 %reduce-scatter.5.cloned.1.call-done = bf16[384,256]{1,0:T(8,128)(2,1)} async-done(((bf16[6144,256]{1,0:T(8,128)(2,1)}), bf16[384,256]{1,0:T(8,128)(2,1)}) %reduce-scatter.5.cloned.1.call-update) | async-done | bytes 196624 | tf_op jit(solution)/shard_map/reduce_scatter | solution.py:27
  (221 shorter events, 109.0 us)
Async XLA Ops:
  7.2 31.3 %all-gather.3.cloned.1.call-start = ((), (), s32[]{:S(2)}) async-start(), calls=%async_computation.2 | async-start | bytes 1769472 | tf_op jit(solution)/shard_map/all_gather | solution.py:23
  9.0 235.0 %reduce-scatter.3.cloned.1.call-start = ((), (), s32[]{:S(2)}) async-start(), calls=%async_computation.3 | async-start | bytes 3342336 | tf_op jit(solution)/shard_map/reduce_scatter | solution.py:27
  38.5 2.0 copy-start
  170.1 73.8 %copy-start.4 = (s32[384]{0:T(512)S(1)}, s32[384]{0:T(512)}, u32[]{:S(2)}) copy-start(s32[384]{0:T(512)} %param.13) | copy-start | bytes 4612
  170.1 102.0 %all-gather.5.cloned.1.call-start = ((), (), s32[]{:S(2)}) async-start(), calls=%async_computation.4 | async-start | bytes 1769472 | tf_op jit(solution)/shard_map/all_gather | solution.py:23
  245.6 231.9 %copy-start.3 = (bf16[384,256]{1,0:T(8,128)(2,1)}, bf16[384,256]{1,0:T(8,128)(2,1)S(1)}, u32[]{:S(2)}) copy-start(bf16[384,256]{1,0:T(8,128)(2,1)S(1)} %get-tuple-element.112) | copy-start | bytes 589828
  245.7 231.9 %reduce-scatter.5.cloned.1.call-start = ((), (), s32[]{:S(2)}) async-start(), calls=%async_computation.5 | async-start | bytes 3342336 | tf_op jit(solution)/shard_map/reduce_scatter | solution.py:27
  272.1 2.0 copy-start.1
  403.8 73.8 %copy-start.2 = (bf16[384,256]{1,0:T(8,128)(2,1)S(1)}, bf16[384,256]{1,0:T(8,128)(2,1)}, u32[]{:S(2)}) copy-start(bf16[384,256]{1,0:T(8,128)(2,1)} %param.12) | copy-start | bytes 589828
Sparse Core Ops, SparseCore 0:
  10.3 28.1 all-gather.2
  170.3 73.6 reduce-scatter.2
  246.2 25.8 all-gather.4
  403.9 73.5 reduce-scatter.4
where the time goes:
time: 490 us; the launch traced here: 486 us
  waiting for transfers between devices  203 us (41%)
  matrix products  169 us (34%)
  other arithmetic  50.6 us (10%)
  local copies, waits for them, and re-layouts  47.8 us (10%)
  between operations  13.8 us (3%)
    reduce_scatter x2, waiting for transfers between devices, propagate(): lax.psum_scatter(flat_terms.astype(jnp.bfloat16), 'row', scatter_dimensio...  147 us
    dot_general x32, matrix products, group_term(): jnp.einsum('tb,tjc->bjc', weights, products, precision=lax.Precision.HIGH...  112 us
    dot_general x32, matrix products, group_term(): jnp.einsum('tij,tic->tjc', tile_block, picked, preferred_element_type=jnp...  57 us
    all_gather x2, waiting for transfers between devices, propagate(): gathered = lax.all_gather(labels, 'col', axis=0, tiled=True)  55.9 us
    eq x32, other arithmetic, group_term(): col_ids[:, None] == jnp.arange(blocks, dtype=jnp.int32)[None, :]  22.9 us
    dynamic_update_slice x32, local copies, waits for them, and re-layouts, propagate(): lax.map(lambda tile_item: group_term(sources, blocks, tile_item), tile_set)  22.4 us
    and x32, other arithmetic, group_term(): picked = jnp.take(sources, row_ids, axis=0)  22.3 us
    gather x32, local copies, waits for them, and re-layouts, group_term(): picked = jnp.take(sources, row_ids, axis=0)  20.7 us
  transfers between devices with their start and end apart: 4, of which 4 were waited for; matrix products, arithmetic and copies ran while one was open for 0% of the time, Pallas kernels for 0%

commit v1 on v0

v1 whole, which is shorter than its diff:
```python
import functools

import jax
import jax.numpy as jnp
from jax import lax
from jax.experimental import pallas as pl
from jax.experimental.pallas import tpu as pltpu
from jax.sharding import PartitionSpec as P

ALPHA = 0.9
MESH = pl.DeviceIdType.MESH
F32 = jnp.float32
BF16 = jnp.bfloat16
RING = 4
TN = (((0,), (0,)), ((), ()))
N_REDUCE = 20
N_GATHER = 13


def sorted_slots(rows, cols, scale):
    groups, slots = rows.shape
    index = jnp.arange(slots, dtype=jnp.int32)[None, :]
    keys = cols * slots + index
    rank = jnp.sum((keys[:, None, :] < keys[:, :, None]).astype(jnp.int32), axis=2)
    placed = rank[:, :, None] == jnp.arange(slots, dtype=jnp.int32)[None, None, :]
    tile = jnp.arange(groups, dtype=jnp.int32)[:, None] * slots + index
    parts = [jnp.sum(jnp.where(placed, v[:, :, None], 0), axis=1) for v in (tile, rows, scale)]
    first = jnp.sum((cols < 1).astype(jnp.int32), axis=1, keepdims=True)
    second = jnp.sum((cols < 2).astype(jnp.int32), axis=1, keepdims=True)
    return jnp.concatenate(parts + [first, second], axis=1)


def kernel(
    cot_ref, seed_ref, order, tiles_hbm,
    first_ref, label_ref,
    tiles, gathered0, gathered1, prefix0, prefix1, current, own, sent, got, keep,
    tile_sem, send_sem, recv_sem,
):
    tile = tiles.shape[1]
    groups = order.shape[0]
    slots = tiles.shape[0] // groups
    gathered = (gathered0, gathered1)
    prefix = (prefix0, prefix1)
    sub = gathered0.shape[1]
    segment, classes = cot_ref.shape
    half = segment // 2
    per = segment // sub
    row, col = lax.axis_index("row"), lax.axis_index("col")
    y, x = row // RING, row % RING
    z, core = col // 2, col % 2
    a = x + core * (y - x)
    b = y + core * (x - y)
    step_a = 1 + 3 * core
    step_b = 4 - 3 * core

    def at(da, db):
        return ((a + da) % RING) * step_a + ((b + db) % RING) * step_b

    def device(da, db):
        return {"row": at(da, db), "col": col}

    a_right, a_left = device(1, 0), device(3, 0)
    b_right, b_left = device(0, 1), device(0, 3)
    z_right = {"row": row, "col": ((z + 1) % RING) * 2 + core}
    z_left = {"row": row, "col": ((z + 3) % RING) * 2 + core}
    twin = {"row": row, "col": z * 2 + (1 - core)}

    loads = [
        pltpu.make_async_copy(
            tiles_hbm.at[pl.ds(q * tiles.shape[0] // 4, tiles.shape[0] // 4)],
            tiles.at[pl.ds(q * tiles.shape[0] // 4, tiles.shape[0] // 4)],
            tile_sem.at[q],
        )
        for q in range(4)
    ]
    for load in loads:
        load.start()

    barrier = pltpu.get_barrier_semaphore()
    for other in (a_right, a_left, b_right, b_left, z_right, z_left, twin):
        pl.semaphore_signal(barrier, inc=1, device_id=other, device_id_type=MESH)

    for block in range(segment // tile):
        seeds = jnp.broadcast_to(seed_ref[block : block + 1, :], (tile, tile)).T
        lanes = lax.broadcasted_iota(jnp.int32, (tile, tile), 1)
        rows = slice(block * tile, (block + 1) * tile)
        for c in range(classes // tile):
            lane = slice(c * tile, (c + 1) * tile)
            kept = jnp.where(seeds == lanes + c * tile, 0.0, 1.0)
            keep[rows, lane] = kept
            masked = (cot_ref[rows, lane].astype(F32) * kept).astype(BF16)
            for part in range(tile // sub):
                gathered0[col * per + block * (tile // sub) + part, :, lane] = masked[part * sub : (part + 1) * sub]

    pl.semaphore_wait(barrier, 7)

    def gather_copy(p, j):
        seg_left = ((z + 3) % RING) * 2 + core
        seg_right = ((z + 1) % RING) * 2 + core
        seg_far = ((z + 2) % RING) * 2 + core
        seg, top, size, target = (
            (col, 0, half, z_right),
            (col, half, half, z_right),
            (col, half, half, z_left),
            (col, 0, half, z_left),
            (seg_left, 0, half, z_right),
            (seg_right, half, half, z_left),
            (col, 0, segment, twin),
            (seg_left, 0, half, twin),
            (seg_left, half, half, twin),
            (seg_right, half, half, twin),
            (seg_right, 0, half, twin),
            (seg_far, 0, half, twin),
            (seg_far, half, half, twin),
        )[j]
        window = gathered[p].at[pl.ds(seg * per + top // sub, size // sub)]
        sem = N_REDUCE + j
        return pltpu.make_async_remote_copy(
            src_ref=window, dst_ref=window, send_sem=send_sem.at[p, sem], recv_sem=recv_sem.at[p, sem],
            device_id=target, device_id_type=MESH,
        )

    def arrival(p, j):
        seg_left = ((z + 3) % RING) * 2 + core
        seg_right = ((z + 1) % RING) * 2 + core
        seg_far = ((z + 2) % RING) * 2 + core
        flip = 1 - 2 * core
        seg, top, size = (
            (seg_left, 0, half),
            (seg_left, half, half),
            (seg_right, half, half),
            (seg_right, 0, half),
            (seg_far, 0, half),
            (seg_far, half, half),
            (col + flip, 0, segment),
            (seg_left + flip, 0, half),
            (seg_left + flip, half, half),
            (seg_right + flip, half, half),
            (seg_right + flip, 0, half),
            (seg_far + flip, 0, half),
            (seg_far + flip, half, half),
        )[j]
        window = gathered[p].at[pl.ds(seg * per + top // sub, size // sub)]
        sem = N_REDUCE + j
        return pltpu.make_async_remote_copy(
            src_ref=window, dst_ref=window, send_sem=send_sem.at[p, sem], recv_sem=recv_sem.at[p, sem],
            device_id=twin, device_id_type=MESH,
        )

    def reduce_copy(p, i, kind, right, left):
        piece = max(kind - 1, 0)
        rows = (pl.ds(0, half), pl.ds(half, half), pl.ds(0, segment), pl.ds(0, segment))[kind]
        sem = 4 * i + kind
        return pltpu.make_async_remote_copy(
            src_ref=sent.at[p, 3 * i + piece, rows], dst_ref=got.at[p, 3 * i + piece, rows],
            send_sem=send_sem.at[p, sem], recv_sem=recv_sem.at[p, sem],
            device_id=(right, left, right, left)[kind], device_id_type=MESH,
        )

    def start_gather(p):
        for j in (0, 2, 6, 1, 3):
            gather_copy(p, j).start()

    def finish_gather(p):
        arrival(p, 0).wait_recv()
        gather_copy(p, 4).start()
        gather_copy(p, 7).start()
        arrival(p, 2).wait_recv()
        gather_copy(p, 5).start()
        gather_copy(p, 9).start()
        arrival(p, 1).wait_recv()
        gather_copy(p, 8).start()
        arrival(p, 3).wait_recv()
        gather_copy(p, 10).start()
        arrival(p, 4).wait_recv()
        gather_copy(p, 11).start()
        arrival(p, 5).wait_recv()
        gather_copy(p, 12).start()
        for j in range(6, N_GATHER):
            arrival(p, j).wait_recv()

    start_gather(0)

    def product(p, u, target):
        total = jnp.zeros((tile, classes), F32)
        prefix[u][0] = total
        for q in range(slots):
            source = order[target, slots + q] * (tile // sub)
            labels = jnp.concatenate([gathered[p][source + part] for part in range(tile // sub)], axis=0)
            term = lax.dot_general(tiles[order[target, q]], labels, TN, preferred_element_type=F32)
            total = total + term * order[target, 2 * slots + q].astype(F32)
            prefix[u][q + 1] = total
        one = prefix[u][order[target, 3 * slots]]
        two = prefix[u][order[target, 3 * slots + 1]]
        current[u, 0:tile] = one
        current[u, tile : 2 * tile] = two - one
        current[u, 2 * tile : 3 * tile] = total - two

    upper, lower, whole = pl.ds(0, half), pl.ds(half, half), pl.ds(0, segment)

    def summed(p, i):
        reduce_copy(p, i, 2, a_right, a_left).wait_recv()
        reduce_copy(p, i, 3, a_right, a_left).wait_recv()
        return own[i] + got[p, 3 * i + 1].astype(F32) + got[p, 3 * i + 2].astype(F32)

    for p in range(2):
        finish_gather(p)
        if p == 0:
            for load in loads:
                load.wait()

        def one_step(s, carry):
            far = s < 2
            side = jnp.logical_and(s >= 2, s < 6)
            i0 = jnp.where(far, 2 * s, jnp.where(side, s - 2, 2 * s - 12))
            i1 = jnp.where(side, i0, i0 + 1)
            da0 = jnp.where(far, 2, jnp.where(side, 1, 0))
            da1 = jnp.where(far, 2, jnp.where(side, 3, 0))
            product(p, 0, at(da0, 2 + i0 * (i0 + 1) // 2))
            product(p, 1, at(da1, 2 + i1 * (i1 + 1) // 2))

            @pl.when(far)
            def _():
                for u in range(2):
                    i = 2 * s + u
                    sent[p, 3 * i] = current[u].astype(BF16)
                    reduce_copy(p, i, 0, a_right, a_left).start()
                    reduce_copy(p, i, 1, a_right, a_left).start()

            @pl.when(side)
            def _():
                i = s - 2
                sent[p, 3 * i + 1, half:segment] = current[0, half:segment].astype(BF16)
                sent[p, 3 * i + 2, 0:half] = current[1, 0:half].astype(BF16)
                reduce_copy(p, i, 0, a_right, a_left).wait_recv()
                sent[p, 3 * i + 1, 0:half] = (current[0, 0:half] + got[p, 3 * i, 0:half].astype(F32)).astype(BF16)
                reduce_copy(p, i, 2, a_right, a_left).start()
                reduce_copy(p, i, 1, a_right, a_left).wait_recv()
                sent[p, 3 * i + 2, half:segment] = (
                    current[1, half:segment] + got[p, 3 * i, half:segment].astype(F32)
                ).astype(BF16)
                reduce_copy(p, i, 3, a_right, a_left).start()

            @pl.when(s >= 6)
            def _():
                own[2 * s - 12] = current[0]
                own[2 * s - 11] = current[1]

            @pl.when(s == 6)
            def _():
                sent[p, 12] = summed(p, 0).astype(BF16)
                reduce_copy(p, 4, 0, b_right, b_left).start()
                reduce_copy(p, 4, 1, b_right, b_left).start()

            return carry

        lax.fori_loop(0, 8, one_step, 0)

        total = summed(p, 1)
        reduce_copy(p, 4, 1, b_right, b_left).wait_recv()
        sent[p, 14, 0:half] = total[0:half].astype(BF16)
        sent[p, 14, half:segment] = (total[half:segment] + got[p, 12, half:segment].astype(F32)).astype(BF16)
        reduce_copy(p, 4, 3, b_right, b_left).start()
        total = summed(p, 2)
        reduce_copy(p, 4, 0, b_right, b_left).wait_recv()
        sent[p, 13, half:segment] = total[half:segment].astype(BF16)
        sent[p, 13, 0:half] = (total[0:half] + got[p, 12, 0:half].astype(F32)).astype(BF16)
        reduce_copy(p, 4, 2, b_right, b_left).start()
        own[3] = summed(p, 3)
        reduce_copy(p, 4, 2, b_right, b_left).wait_recv()
        reduce_copy(p, 4, 3, b_right, b_left).wait_recv()
        own[3] = ALPHA * (own[3] + got[p, 13].astype(F32) + got[p, 14].astype(F32))

        if p == 0:
            first = own[3].astype(BF16)
            first_ref[...] = first
            masked = (first.astype(F32) * keep[...]).astype(BF16)
            for part in range(per):
                gathered1[col * per + part] = masked[part * sub : (part + 1) * sub]
            start_gather(1)
        else:
            label_ref[...] = (
                own[3] + (1.0 - ALPHA) * keep[...] * (cot_ref[...].astype(F32) + first_ref[...].astype(F32))
            ).astype(BF16)

    for p in range(2):
        for j in range(N_GATHER):
            gather_copy(p, j).wait_send()
        for i in range(5):
            right, left = (a_right, a_left) if i < 4 else (b_right, b_left)
            for kind in range(4):
                reduce_copy(p, i, kind, right, left).wait_send()


def local(cotangent, seed_label, tile_values, tile_rows, tile_cols, tile_scale):
    segment, classes = cotangent.shape
    _, _, groups, slots, tile, _ = tile_values.shape
    vmem, smem = pl.BlockSpec(memory_space=pltpu.VMEM), pl.BlockSpec(memory_space=pltpu.SMEM)
    out = jax.ShapeDtypeStruct((segment, classes), BF16)
    return pl.pallas_call(
        kernel,
        out_shape=(out, out),
        in_specs=[vmem, vmem, smem, pl.BlockSpec(memory_space=pl.ANY)],
        out_specs=(vmem, vmem),
        scratch_shapes=[
            pltpu.VMEM((groups * slots, tile, tile), BF16),
            pltpu.VMEM((2 * RING * segment // 64, 64, classes), BF16),
            pltpu.VMEM((2 * RING * segment // 64, 64, classes), BF16),
            pltpu.VMEM((slots + 1, tile, classes), F32),
            pltpu.VMEM((slots + 1, tile, classes), F32),
            pltpu.VMEM((2, segment, classes), F32),
            pltpu.VMEM((4, segment, classes), F32),
            pltpu.VMEM((2, 15, segment, classes), BF16),
            pltpu.VMEM((2, 15, segment, classes), BF16),
            pltpu.VMEM((segment, classes), F32),
            pltpu.SemaphoreType.DMA((4,)),
            pltpu.SemaphoreType.DMA((2, N_REDUCE + N_GATHER)),
            pltpu.SemaphoreType.DMA((2, N_REDUCE + N_GATHER)),
        ],
        compiler_params=pltpu.CompilerParams(
            collective_id=0, has_side_effects=True, vmem_limit_bytes=56 * 1024 * 1024
        ),
        name="propagate_twice",
    )(
        cotangent,
        seed_label.reshape(segment // tile, tile),
        sorted_slots(tile_rows[0, 0], tile_cols[0, 0], tile_scale[0, 0]),
        tile_values.reshape(groups * slots, tile, tile),
    )


def solution(mesh):
    return jax.shard_map(
        local,
        mesh=mesh,
        in_specs=(
            P(("row", "col"), None),
            P(("row", "col")),
            P("row", "col", None, None, None, None),
            P("row", "col", None, None),
            P("row", "col", None, None),
            P("row", "col", None, None),
        ),
        out_specs=(P(("row", "col"), None), P(("row", "col"), None)),
        check_vma=False,
    )
```

time: 490 us -> 79.4 us (0.16)
  waiting for transfers between devices: 203 us -> 0 us
  matrix products: 169 us -> 0 us
  Pallas kernels: 0 us -> 71.3 us
  other arithmetic: 50.6 us -> 3.04 us
  local copies, waits for them, and re-layouts: 47.8 us -> 4.08 us
  between operations: 13.8 us -> 0.66 us
    dot_general x64 -> x0, matrix products: 169 us -> none  [the longest x32 112 us: group_term(): jnp.einsum('tb,tjc->bjc', weights, products, precision=lax.Precision.HIGH...]
    reduce_scatter x2 -> x0, waiting for transfers between devices: 147 us -> none  [propagate(): lax.psum_scatter(flat_terms.astype(jnp.bfloat16), 'row', scatter_dimensio...]
    pallas_call x0 -> x1, Pallas kernels: none -> 71.3 us  [local(): pl.pallas_call(kernel, out_shape=(out, out), in_specs=[vmem, vmem, smem,...]
    all_gather x2 -> x0, waiting for transfers between devices: 55.9 us -> none  [propagate(): gathered = lax.all_gather(labels, 'col', axis=0, tiled=True)]
    eq x32 -> x0, other arithmetic: 22.9 us -> none  [group_term(): col_ids[:, None] == jnp.arange(blocks, dtype=jnp.int32)[None, :]]
    dynamic_update_slice x32 -> x0, local copies, waits for them, and re-layouts: 22.4 us -> none  [propagate(): lax.map(lambda tile_item: group_term(sources, blocks, tile_item), tile_set)]
    and x32 -> x0, other arithmetic: 22.3 us -> none  [group_term(): picked = jnp.take(sources, row_ids, axis=0)]
    gather x32 -> x0, local copies, waits for them, and re-layouts: 20.7 us -> none  [group_term(): picked = jnp.take(sources, row_ids, axis=0)]
  transfers between devices with their start and end apart: 4 -> 0, of which waited for: 4 -> 0; matrix products, arithmetic and copies ran while one was open for 0% -> 0% of each run, Pallas kernels for 0% -> 0%
where the time goes in v1:
time: 79.4 us; the launch traced here: 79.1 us
  Pallas kernels  71.3 us (90%)
  local copies, waits for them, and re-layouts  4.08 us (5%)
  other arithmetic  3.04 us (4%)
    pallas_call x1, Pallas kernels, local(): pl.pallas_call(kernel, out_shape=(out, out), in_specs=[vmem, vmem, smem,...  71.3 us
    unnamed x2, local copies, waits for them, and re-layouts  3.23 us

profile of v1, /device:TPU:1, one launch (start us, length us, event | category | flops | bytes accessed | tf_op | source)
XLA Modules:
  0.0 79.1 jit_solution(18126485498650820152)
XLA Ops:
  0.6 0.8 %convert_reduce_fusion.1 = (s32[16]{0:T(128)S(1)}, s32[16]{0:T(128)S(1)}) fusion(s32[1,1,16,24]{3,2,1,0:T(8,128)} %param.10), kind=kLoop, calls=%fused_computation.6 | loop fusion | flops 2272 | bytes 1664 | tf_op jit(solution)/shard_map/reduce_sum | solution.py:29
  1.5 0.1 copy.10
  1.5 0.1 copy.11
  1.6 0.1 iota_add_fusion
  1.7 0.7 bitcast_add_fusion
  2.4 0.4 convert_reduce_fusion
  2.8 1.0 %select_reduce_fusion = (s32[16,24]{1,0:T(8,128)S(1)}, s32[16,24]{1,0:T(8,128)S(1)}, s32[16,24]{1,0:T(8,128)S(1)}) fusion(s32[16,24]{1,0:T(8,128)} %bitcast.9, s32[16,24]{1,0:T(8,128)S(1)} %convert_reduce_fusion, s32[16,24]{1,0:T(8,128)} %bitcast.10, s32[16,24]{1,0:T(8,128)S(1)} %iota_add_fusion), kind=kLoop, calls=%fused_computation | loop fusion | flops 63360 | bytes 10752 | tf_op jit(solution)/shard_map/reduce_sum | solution.py:27
  3.9 0.7 concatenate.3.order
  4.5 71.3 %propagate_twice.1 = (bf16[384,256]{1,0:T(8,128)(2,1)}, bf16[384,256]{1,0:T(8,128)(2,1)}) custom-call(bf16[384,256]{1,0:T(8,128)(2,1)} %cot_ref.1, s32[3,128]{1,0:T(4,128)} %bitcast.11, s32[16,74]{1,0:T(8,128)} %concatenate.3.order, bf16[384,128,128]{2,1,0:T(8,128)(2,1)} %bitcast.8), custom_call_target="tpu_custom_call" | custom-call | tf_op jit(solution)/shard_map/propagate_twice/pallas_call | solution.py:300
  75.8 1.6 %copy.14 = bf16[384,256]{1,0:T(8,128)(2,1)} copy(bf16[384,256]{1,0:T(8,128)(2,1)} %get-tuple-element.9) | data formatting | bytes 393216
  77.5 1.6 %copy.15 = bf16[384,256]{1,0:T(8,128)(2,1)} copy(bf16[384,256]{1,0:T(8,128)(2,1)} %get-tuple-element.10) | data formatting | bytes 393216
  (1 shorter events, 0.0 us)

commit v2 on v1

--- a/solution.py
+++ b/solution.py
@@ -17,27 +17,32 @@
 N_GATHER = 13
 
 
-def sorted_slots(rows, cols, scale):
-    groups, slots = rows.shape
-    index = jnp.arange(slots, dtype=jnp.int32)[None, :]
-    keys = cols * slots + index
-    rank = jnp.sum((keys[:, None, :] < keys[:, :, None]).astype(jnp.int32), axis=2)
-    placed = rank[:, :, None] == jnp.arange(slots, dtype=jnp.int32)[None, None, :]
-    tile = jnp.arange(groups, dtype=jnp.int32)[:, None] * slots + index
-    parts = [jnp.sum(jnp.where(placed, v[:, :, None], 0), axis=1) for v in (tile, rows, scale)]
-    first = jnp.sum((cols < 1).astype(jnp.int32), axis=1, keepdims=True)
-    second = jnp.sum((cols < 2).astype(jnp.int32), axis=1, keepdims=True)
-    return jnp.concatenate(parts + [first, second], axis=1)
+def sort_network(count):
+    size = 1
+    while size < count:
+        size *= 2
+    pairs = []
+    p = 1
+    while p < size:
+        k = p
+        while k >= 1:
+            for j in range(k % p, size - k, 2 * k):
+                for i in range(min(k, size - j - k)):
+                    if (i + j) // (p * 2) == (i + j + k) // (p * 2) and i + j + k < count:
+                        pairs.append((i + j, i + j + k))
+            k //= 2
+        p *= 2
+    return pairs
 
 
 def kernel(
-    cot_ref, seed_ref, order, tiles_hbm,
+    cot_ref, seed_ref, rows_ref, cols_ref, scale_ref, tiles_hbm,
     first_ref, label_ref,
-    tiles, gathered0, gathered1, prefix0, prefix1, current, own, sent, got, keep,
+    tiles, gathered0, gathered1, prefix0, prefix1, current, own, sent, got, keep, order,
     tile_sem, send_sem, recv_sem,
 ):
     tile = tiles.shape[1]
-    groups = order.shape[0]
+    groups = rows_ref.shape[0]
     slots = tiles.shape[0] // groups
     gathered = (gathered0, gathered1)
     prefix = (prefix0, prefix1)
@@ -181,6 +186,25 @@
 
     start_gather(0)
 
+    def sort_group(g, carry):
+        keys, first, second = [], 0, 0
+        for k in range(slots):
+            c = cols_ref[g, k]
+            keys.append(c * 8192 + (k * 256 + rows_ref[g, k] * 8 + scale_ref[g, k]))
+            first = first + ((2 - c) >> 1)
+            second = second + (1 - (c >> 1))
+        for i, j in sort_network(slots):
+            keys[i], keys[j] = jnp.minimum(keys[i], keys[j]), jnp.maximum(keys[i], keys[j])
+        for k in range(slots):
+            order[g, k] = ((keys[k] >> 8) & 31) + g * slots
+            order[g, slots + k] = (keys[k] >> 3) & 31
+            order[g, 2 * slots + k] = keys[k] & 7
+        order[g, 3 * slots] = first
+        order[g, 3 * slots + 1] = second
+        return carry
+
+    lax.fori_loop(0, groups, sort_group, 0)
+
     def product(p, u, target):
         total = jnp.zeros((tile, classes), F32)
         prefix[u][0] = total
@@ -300,7 +324,7 @@
     return pl.pallas_call(
         kernel,
         out_shape=(out, out),
-        in_specs=[vmem, vmem, smem, pl.BlockSpec(memory_space=pl.ANY)],
+        in_specs=[vmem, vmem, smem, smem, smem, pl.BlockSpec(memory_space=pl.ANY)],
         out_specs=(vmem, vmem),
         scratch_shapes=[
             pltpu.VMEM((groups * slots, tile, tile), BF16),
@@ -313,6 +337,7 @@
             pltpu.VMEM((2, 15, segment, classes), BF16),
             pltpu.VMEM((2, 15, segment, classes), BF16),
             pltpu.VMEM((segment, classes), F32),
+            pltpu.SMEM((groups, 3 * slots + 2), jnp.int32),
             pltpu.SemaphoreType.DMA((4,)),
             pltpu.SemaphoreType.DMA((2, N_REDUCE + N_GATHER)),
             pltpu.SemaphoreType.DMA((2, N_REDUCE + N_GATHER)),
@@ -324,7 +349,9 @@
     )(
         cotangent,
         seed_label.reshape(segment // tile, tile),
-        sorted_slots(tile_rows[0, 0], tile_cols[0, 0], tile_scale[0, 0]),
+        tile_rows[0, 0],
+        tile_cols[0, 0],
+        tile_scale[0, 0],
         tile_values.reshape(groups * slots, tile, tile),
     )
 

time: 79.4 us -> 75.6 us (0.952)
  other arithmetic: 3.04 us -> 0 us
  local copies, waits for them, and re-layouts: 4.08 us -> 3.23 us
    reduce_sum x3 -> x0, other arithmetic: 2.26 us -> none  [the longest x1 1 us: sorted_slots(): jnp.sum(jnp.where(placed, v[:, :, None], 0), axis=1)]
where the time goes in v2:
time: 75.6 us; the launch traced here: 75.4 us
  Pallas kernels  71.5 us (95%)
  local copies, waits for them, and re-layouts  3.23 us (4%)
    pallas_call x1, Pallas kernels, local(): pl.pallas_call(kernel, out_shape=(out, out), in_specs=[vmem, vmem, smem,...  71.5 us
    unnamed x2, local copies, waits for them, and re-layouts  3.23 us

profile of v2, /device:TPU:1, one launch (start us, length us, event | category | flops | bytes accessed | tf_op | source)
XLA Modules:
  0.0 75.4 jit_solution(1414145345573343261)
XLA Ops:
  0.6 71.5 %propagate_twice.1 = (bf16[384,256]{1,0:T(8,128)(2,1)}, bf16[384,256]{1,0:T(8,128)(2,1)}) custom-call(bf16[384,256]{1,0:T(8,128)(2,1)} %cot_ref.1, s32[3,128]{1,0:T(4,128)} %bitcast.9, s32[16,24]{1,0:T(8,128)} %bitcast.6, s32[16,24]{1,0:T(8,128)} %bitcast.7, s32[16,24]{1,0:T(8,128)} %bitcast.8, bf16[384,128,128]{2,1,0:T(8,128)(2,1)} %bitcast.5), custom_call_target="tpu_custom_call" | custom-call | tf_op jit(solution)/shard_map/propagate_twice/pallas_call | solution.py:324
  72.2 1.6 %copy.10 = bf16[384,256]{1,0:T(8,128)(2,1)} copy(bf16[384,256]{1,0:T(8,128)(2,1)} %get-tuple-element.4) | data formatting | bytes 393216
  73.8 1.6 %copy.11 = bf16[384,256]{1,0:T(8,128)(2,1)} copy(bf16[384,256]{1,0:T(8,128)(2,1)} %get-tuple-element.5) | data formatting | bytes 393216

commit v3 on v2

--- a/solution.py
+++ b/solution.py
@@ -316,12 +316,31 @@
                 reduce_copy(p, i, kind, right, left).wait_send()
 
 
+def hand_over(first_in, label_in, first_out, label_out, held, sem):
+    loads = [
+        pltpu.make_async_copy(first_in, held.at[0], sem.at[0]),
+        pltpu.make_async_copy(label_in, held.at[1], sem.at[1]),
+    ]
+    stores = [
+        pltpu.make_async_copy(held.at[0], first_out, sem.at[2]),
+        pltpu.make_async_copy(held.at[1], label_out, sem.at[3]),
+    ]
+    for load in loads:
+        load.start()
+    for load, store in zip(loads, stores):
+        load.wait()
+        store.start()
+    for store in stores:
+        store.wait()
+
+
 def local(cotangent, seed_label, tile_values, tile_rows, tile_cols, tile_scale):
     segment, classes = cotangent.shape
     _, _, groups, slots, tile, _ = tile_values.shape
     vmem, smem = pl.BlockSpec(memory_space=pltpu.VMEM), pl.BlockSpec(memory_space=pltpu.SMEM)
     out = jax.ShapeDtypeStruct((segment, classes), BF16)
-    return pl.pallas_call(
+    hbm = pl.BlockSpec(memory_space=pl.ANY)
+    results = pl.pallas_call(
         kernel,
         out_shape=(out, out),
         in_specs=[vmem, vmem, smem, smem, smem, pl.BlockSpec(memory_space=pl.ANY)],
@@ -354,6 +373,14 @@
         tile_scale[0, 0],
         tile_values.reshape(groups * slots, tile, tile),
     )
+    return pl.pallas_call(
+        hand_over,
+        out_shape=(out, out),
+        in_specs=[hbm, hbm],
+        out_specs=(hbm, hbm),
+        scratch_shapes=[pltpu.VMEM((2, segment, classes), BF16), pltpu.SemaphoreType.DMA((4,))],
+        name="finish_results",
+    )(*results)
 
 
 def solution(mesh):

time: 75.6 us -> 74.1 us (0.980)
  local copies, waits for them, and re-layouts: 3.23 us -> 0 us
  Pallas kernels: 71.5 us -> 73.3 us
    unnamed x2 -> x0, local copies, waits for them, and re-layouts: 3.23 us -> none
    pallas_call x0 -> x1, Pallas kernels: none -> 1.73 us  [local(): pl.pallas_call(hand_over, out_shape=(out, out), in_specs=[hbm, hbm], out_...]
where the time goes in v3:
time: 74.1 us; the launch traced here: 73.9 us
  Pallas kernels  73.3 us (99%)
    pallas_call x1, Pallas kernels, local(): pl.pallas_call(kernel, out_shape=(out, out), in_specs=[vmem, vmem, smem,...  71.5 us
    pallas_call x1, Pallas kernels, local(): pl.pallas_call(hand_over, out_shape=(out, out), in_specs=[hbm, hbm], out_...  1.73 us

profile of v3, /device:TPU:1, one launch (start us, length us, event | category | flops | bytes accessed | tf_op | source)
XLA Modules:
  0.0 73.9 jit_solution(7977047415629452485)
XLA Ops:
  0.6 71.5 %propagate_twice.1 = (bf16[384,256]{1,0:T(8,128)(2,1)}, bf16[384,256]{1,0:T(8,128)(2,1)}) custom-call(bf16[384,256]{1,0:T(8,128)(2,1)} %cot_ref.1, s32[3,128]{1,0:T(4,128)} %bitcast.9, s32[16,24]{1,0:T(8,128)} %bitcast.6, s32[16,24]{1,0:T(8,128)} %bitcast.7, s32[16,24]{1,0:T(8,128)} %bitcast.8, bf16[384,128,128]{2,1,0:T(8,128)(2,1)} %bitcast.5), custom_call_target="tpu_custom_call" | custom-call | tf_op jit(solution)/shard_map/propagate_twice/pallas_call | solution.py:343
  72.2 1.7 %finish_results.1 = (bf16[384,256]{1,0:T(8,128)(2,1)}, bf16[384,256]{1,0:T(8,128)(2,1)}) custom-call(bf16[384,256]{1,0:T(8,128)(2,1)} %get-tuple-element.4.first_in, bf16[384,256]{1,0:T(8,128)(2,1)} %get-tuple-element.5.label_in), custom_call_target="tpu_custom_call" | custom-call | tf_op jit(solution)/shard_map/finish_results/pallas_call | solution.py:376

commit v4 on v2

--- a/solution.py
+++ b/solution.py
@@ -1,5 +1,3 @@
-import functools
-
 import jax
 import jax.numpy as jnp
 from jax import lax
@@ -13,7 +11,7 @@
 BF16 = jnp.bfloat16
 RING = 4
 TN = (((0,), (0,)), ((), ()))
-N_REDUCE = 20
+N_REDUCE = 30
 N_GATHER = 13
 
 
@@ -36,9 +34,9 @@
 
 
 def kernel(
-    cot_ref, seed_ref, rows_ref, cols_ref, scale_ref, tiles_hbm,
+    cot_hbm, seed_hbm, rows_hbm, cols_hbm, scale_hbm, tiles_hbm,
     first_ref, label_ref,
-    tiles, gathered0, gathered1, prefix0, prefix1, current, own, sent, got, keep, order,
+    cot_ref, seed_ref, rows_ref, cols_ref, scale_ref, small_sem, tiles, gathered0, gathered1, prefix0, prefix1, current, own, sent, got, keep, order,
     tile_sem, send_sem, recv_sem,
 ):
     tile = tiles.shape[1]
@@ -70,6 +68,18 @@
     z_left = {"row": row, "col": ((z + 3) % RING) * 2 + core}
     twin = {"row": row, "col": z * 2 + (1 - core)}
 
+    barrier = pltpu.get_barrier_semaphore()
+    for other in (a_right, a_left, b_right, b_left, z_right, z_left, twin):
+        pl.semaphore_signal(barrier, inc=1, device_id=other, device_id_type=MESH)
+
+    small = [
+        pltpu.make_async_copy(source, target, small_sem.at[q])
+        for q, (source, target) in enumerate((
+            (cot_hbm, cot_ref), (seed_hbm, seed_ref), (rows_hbm, rows_ref), (cols_hbm, cols_ref), (scale_hbm, scale_ref)
+        ))
+    ]
+    for load in small:
+        load.start()
     loads = [
         pltpu.make_async_copy(
             tiles_hbm.at[pl.ds(q * tiles.shape[0] // 4, tiles.shape[0] // 4)],
@@ -81,10 +91,8 @@
     for load in loads:
         load.start()
 
-    barrier = pltpu.get_barrier_semaphore()
-    for other in (a_right, a_left, b_right, b_left, z_right, z_left, twin):
-        pl.semaphore_signal(barrier, inc=1, device_id=other, device_id_type=MESH)
-
+    small[0].wait()
+    small[1].wait()
     for block in range(segment // tile):
         seeds = jnp.broadcast_to(seed_ref[block : block + 1, :], (tile, tile)).T
         lanes = lax.broadcasted_iota(jnp.int32, (tile, tile), 1)
@@ -152,15 +160,23 @@
             device_id=twin, device_id_type=MESH,
         )
 
+    upper, lower = pl.ds(0, half), pl.ds(half, half)
+
     def reduce_copy(p, i, kind, right, left):
-        piece = max(kind - 1, 0)
-        rows = (pl.ds(0, half), pl.ds(half, half), pl.ds(0, segment), pl.ds(0, segment))[kind]
-        sem = 4 * i + kind
+        piece = 3 * i + kind // 2
+        rows = (upper, lower, upper, lower, lower, upper)[kind]
+        sem = 6 * i + kind
         return pltpu.make_async_remote_copy(
-            src_ref=sent.at[p, 3 * i + piece, rows], dst_ref=got.at[p, 3 * i + piece, rows],
+            src_ref=sent.at[p, piece, rows], dst_ref=got.at[p, piece, rows],
             send_sem=send_sem.at[p, sem], recv_sem=recv_sem.at[p, sem],
-            device_id=(right, left, right, left)[kind], device_id_type=MESH,
+            device_id=(right, left, right, right, left, left)[kind], device_id_type=MESH,
         )
+
+    def along_a(p, i, kind):
+        return reduce_copy(p, i, kind, a_right, a_left)
+
+    def along_b(p, kind):
+        return reduce_copy(p, 4, kind, b_right, b_left)
 
     def start_gather(p):
         for j in (0, 2, 6, 1, 3):
@@ -186,6 +202,9 @@
 
     start_gather(0)
 
+    for load in small[2:]:
+        load.wait()
+
     def sort_group(g, carry):
         keys, first, second = [], 0, 0
         for k in range(slots):
@@ -220,12 +239,10 @@
         current[u, tile : 2 * tile] = two - one
         current[u, 2 * tile : 3 * tile] = total - two
 
-    upper, lower, whole = pl.ds(0, half), pl.ds(half, half), pl.ds(0, segment)
-
-    def summed(p, i):
-        reduce_copy(p, i, 2, a_right, a_left).wait_recv()
-        reduce_copy(p, i, 3, a_right, a_left).wait_recv()
-        return own[i] + got[p, 3 * i + 1].astype(F32) + got[p, 3 * i + 2].astype(F32)
+    def summed(p, i, rows, from_left, from_right):
+        along_a(p, i, from_left).wait_recv()
+        along_a(p, i, from_right).wait_recv()
+        return own[i, rows] + got[p, 3 * i + 1, rows].astype(F32) + got[p, 3 * i + 2, rows].astype(F32)
 
     for p in range(2):
         finish_gather(p)
@@ -248,22 +265,24 @@
                 for u in range(2):
                     i = 2 * s + u
                     sent[p, 3 * i] = current[u].astype(BF16)
-                    reduce_copy(p, i, 0, a_right, a_left).start()
-                    reduce_copy(p, i, 1, a_right, a_left).start()
+                    along_a(p, i, 0).start()
+                    along_a(p, i, 1).start()
 
             @pl.when(side)
             def _():
                 i = s - 2
                 sent[p, 3 * i + 1, half:segment] = current[0, half:segment].astype(BF16)
+                along_a(p, i, 3).start()
                 sent[p, 3 * i + 2, 0:half] = current[1, 0:half].astype(BF16)
-                reduce_copy(p, i, 0, a_right, a_left).wait_recv()
+                along_a(p, i, 5).start()
+                along_a(p, i, 0).wait_recv()
                 sent[p, 3 * i + 1, 0:half] = (current[0, 0:half] + got[p, 3 * i, 0:half].astype(F32)).astype(BF16)
-                reduce_copy(p, i, 2, a_right, a_left).start()
-                reduce_copy(p, i, 1, a_right, a_left).wait_recv()
+                along_a(p, i, 2).start()
+                along_a(p, i, 1).wait_recv()
                 sent[p, 3 * i + 2, half:segment] = (
                     current[1, half:segment] + got[p, 3 * i, half:segment].astype(F32)
                 ).astype(BF16)
-                reduce_copy(p, i, 3, a_right, a_left).start()
+                along_a(p, i, 4).start()
 
             @pl.when(s >= 6)
             def _():
@@ -272,61 +291,78 @@
 
             @pl.when(s == 6)
             def _():
-                sent[p, 12] = summed(p, 0).astype(BF16)
-                reduce_copy(p, 4, 0, b_right, b_left).start()
-                reduce_copy(p, 4, 1, b_right, b_left).start()
+                sent[p, 12, upper] = summed(p, 0, upper, 2, 5).astype(BF16)
+                along_b(p, 0).start()
+                sent[p, 12, lower] = summed(p, 0, lower, 3, 4).astype(BF16)
+                along_b(p, 1).start()
 
             return carry
 
         lax.fori_loop(0, 8, one_step, 0)
 
-        total = summed(p, 1)
-        reduce_copy(p, 4, 1, b_right, b_left).wait_recv()
-        sent[p, 14, 0:half] = total[0:half].astype(BF16)
-        sent[p, 14, half:segment] = (total[half:segment] + got[p, 12, half:segment].astype(F32)).astype(BF16)
-        reduce_copy(p, 4, 3, b_right, b_left).start()
-        total = summed(p, 2)
-        reduce_copy(p, 4, 0, b_right, b_left).wait_recv()
-        sent[p, 13, half:segment] = total[half:segment].astype(BF16)
-        sent[p, 13, 0:half] = (total[0:half] + got[p, 12, 0:half].astype(F32)).astype(BF16)
-        reduce_copy(p, 4, 2, b_right, b_left).start()
-        own[3] = summed(p, 3)
-        reduce_copy(p, 4, 2, b_right, b_left).wait_recv()
-        reduce_copy(p, 4, 3, b_right, b_left).wait_recv()
-        own[3] = ALPHA * (own[3] + got[p, 13].astype(F32) + got[p, 14].astype(F32))
-
-        if p == 0:
-            first = own[3].astype(BF16)
-            first_ref[...] = first
-            masked = (first.astype(F32) * keep[...]).astype(BF16)
-            for part in range(per):
-                gathered1[col * per + part] = masked[part * sub : (part + 1) * sub]
-            start_gather(1)
-        else:
-            label_ref[...] = (
-                own[3] + (1.0 - ALPHA) * keep[...] * (cot_ref[...].astype(F32) + first_ref[...].astype(F32))
-            ).astype(BF16)
+        sent[p, 14, upper] = summed(p, 1, upper, 2, 5).astype(BF16)
+        along_b(p, 5).start()
+        sent[p, 13, lower] = summed(p, 2, lower, 3, 4).astype(BF16)
+        along_b(p, 3).start()
+        total = summed(p, 1, lower, 3, 4)
+        along_b(p, 1).wait_recv()
+        sent[p, 14, lower] = (total + got[p, 12, lower].astype(F32)).astype(BF16)
+        along_b(p, 4).start()
+        total = summed(p, 2, upper, 2, 5)
+        along_b(p, 0).wait_recv()
+        sent[p, 13, upper] = (total + got[p, 12, upper].astype(F32)).astype(BF16)
+        along_b(p, 2).start()
+        own[3, upper] = summed(p, 3, upper, 2, 5)
+        own[3, lower] = summed(p, 3, lower, 3, 4)
+        for top, from_left, from_right in ((0, 2, 5), (half, 3, 4)):
+            rows = pl.ds(top, half)
+            along_b(p, from_left).wait_recv()
+            along_b(p, from_right).wait_recv()
+            total = ALPHA * (own[3, rows] + got[p, 13, rows].astype(F32) + got[p, 14, rows].astype(F32))
+            if p == 0:
+                first = total.astype(BF16)
+                masked = (first.astype(F32) * keep[rows]).astype(BF16)
+                for part in range(half // sub):
+                    gathered1[col * per + top // sub + part] = masked[part * sub : (part + 1) * sub]
+                for j in (0,) if top == 0 else (2, 6, 1, 3):
+                    gather_copy(1, j).start()
+                first_ref[rows] = first
+            else:
+                label_ref[rows] = (
+                    total + (1.0 - ALPHA) * keep[rows] * (cot_ref[rows].astype(F32) + first_ref[rows].astype(F32))
+                ).astype(BF16)
 
     for p in range(2):
         for j in range(N_GATHER):
             gather_copy(p, j).wait_send()
-        for i in range(5):
-            right, left = (a_right, a_left) if i < 4 else (b_right, b_left)
-            for kind in range(4):
-                reduce_copy(p, i, kind, right, left).wait_send()
+        for kind in range(6):
+            for i in range(4):
+                along_a(p, i, kind).wait_send()
+            along_b(p, kind).wait_send()
+
+
+def hand_over(first_in, label_in, first_out, label_out):
+    first_out[...] = first_in[...]
+    label_out[...] = label_in[...]
 
 
 def local(cotangent, seed_label, tile_values, tile_rows, tile_cols, tile_scale):
     segment, classes = cotangent.shape
     _, _, groups, slots, tile, _ = tile_values.shape
-    vmem, smem = pl.BlockSpec(memory_space=pltpu.VMEM), pl.BlockSpec(memory_space=pltpu.SMEM)
+    vmem = pl.BlockSpec(memory_space=pltpu.VMEM)
     out = jax.ShapeDtypeStruct((segment, classes), BF16)
-    return pl.pallas_call(
+    results = pl.pallas_call(
         kernel,
         out_shape=(out, out),
-        in_specs=[vmem, vmem, smem, smem, smem, pl.BlockSpec(memory_space=pl.ANY)],
+        in_specs=[pl.BlockSpec(memory_space=pltpu.HBM)] * 6,
         out_specs=(vmem, vmem),
         scratch_shapes=[
+            pltpu.VMEM((segment, classes), BF16),
+            pltpu.VMEM((segment // tile, tile), jnp.int32),
+            pltpu.SMEM((groups, slots), jnp.int32),
+            pltpu.SMEM((groups, slots), jnp.int32),
+            pltpu.SMEM((groups, slots), jnp.int32),
+            pltpu.SemaphoreType.DMA((5,)),
             pltpu.VMEM((groups * slots, tile, tile), BF16),
             pltpu.VMEM((2 * RING * segment // 64, 64, classes), BF16),
             pltpu.VMEM((2 * RING * segment // 64, 64, classes), BF16),
@@ -343,17 +379,25 @@
             pltpu.SemaphoreType.DMA((2, N_REDUCE + N_GATHER)),
         ],
         compiler_params=pltpu.CompilerParams(
-            collective_id=0, has_side_effects=True, vmem_limit_bytes=56 * 1024 * 1024
+            collective_id=0, has_side_effects=True, vmem_limit_bytes=42 * 1024 * 1024
         ),
         name="propagate_twice",
     )(
-        cotangent,
-        seed_label.reshape(segment // tile, tile),
-        tile_rows[0, 0],
-        tile_cols[0, 0],
-        tile_scale[0, 0],
+        pltpu.with_memory_space_constraint(cotangent, pltpu.HBM),
+        pltpu.with_memory_space_constraint(seed_label.reshape(segment // tile, tile), pltpu.HBM),
+        pltpu.with_memory_space_constraint(tile_rows[0, 0], pltpu.HBM),
+        pltpu.with_memory_space_constraint(tile_cols[0, 0], pltpu.HBM),
+        pltpu.with_memory_space_constraint(tile_scale[0, 0], pltpu.HBM),
         tile_values.reshape(groups * slots, tile, tile),
     )
+    return pl.pallas_call(
+        hand_over,
+        out_shape=(out, out),
+        in_specs=[vmem, vmem],
+        out_specs=(vmem, vmem),
+        compiler_params=pltpu.CompilerParams(vmem_limit_bytes=4 * 1024 * 1024),
+        name="finish_results",
+    )(*results)
 
 
 def solution(mesh):

time: 75.6 us -> 71.3 us (0.943)
  local copies, waits for them, and re-layouts: 3.23 us -> 0 us
  Pallas kernels: 71.5 us -> 70.6 us
    unnamed x2 -> x0, local copies, waits for them, and re-layouts: 3.23 us -> none
    pallas_call x1 -> x2, Pallas kernels: 71.5 us -> 70.6 us  [the longest x1 69.8 us: local(): pl.pallas_call(kernel, out_shape=(out, out), in_specs=[pl.BlockSpec(memor...]
where the time goes in v4:
time: 71.3 us; the launch traced here: 71.2 us
  Pallas kernels  70.6 us (99%)
    pallas_call x1, Pallas kernels, local(): pl.pallas_call(kernel, out_shape=(out, out), in_specs=[pl.BlockSpec(memor...  69.8 us

profile of v4, /device:TPU:1, one launch (start us, length us, event | category | flops | bytes accessed | tf_op | source)
XLA Modules:
  0.0 71.2 jit_solution(8854541560417757182)
XLA Ops:
  0.6 69.8 %propagate_twice.1 = (bf16[384,256]{1,0:T(8,128)(2,1)S(1)}, bf16[384,256]{1,0:T(8,128)(2,1)S(1)}) custom-call(bf16[384,256]{1,0:T(8,128)(2,1)} %cot_hbm.1, s32[3,128]{1,0:T(4,128)} %bitcast.9, s32[16,24]{1,0:T(8,128)} %bitcast.6, s32[16,24]{1,0:T(8,128)} %bitcast.7, s32[16,24]{1,0:T(8,128)} %bitcast.8, bf16[384,128,128]{2,1,0:T(8,128)(2,1)} %bitcast.5), custom_call_target="tpu_custom_call" | custom-call | tf_op jit(solution)/shard_map/propagate_twice/pallas_call | solution.py:354
  70.5 0.8 %finish_results.1 = (bf16[384,256]{1,0:T(8,128)(2,1)}, bf16[384,256]{1,0:T(8,128)(2,1)}) custom-call(bf16[384,256]{1,0:T(8,128)(2,1)S(1)} %get-tuple-element.4.first_in, bf16[384,256]{1,0:T(8,128)(2,1)S(1)} %get-tuple-element.5.label_in), custom_call_target="tpu_custom_call" | custom-call | tf_op jit(solution)/shard_map/finish_results/pallas_call | solution.py:393

commit v5 on v4

--- a/solution.py
+++ b/solution.py
@@ -250,6 +250,15 @@
             for load in loads:
                 load.wait()
 
+        def send_whole(u, i):
+            sent[p, 3 * i] = current[u].astype(BF16)
+            along_a(p, i, 0).start()
+            along_a(p, i, 1).start()
+
+        for i in range(2):
+            product(p, i, at(2, 2 + i * (i + 1) // 2))
+            send_whole(i, i)
+
         def one_step(s, carry):
             far = s < 2
             side = jnp.logical_and(s >= 2, s < 6)
@@ -263,10 +272,7 @@
             @pl.when(far)
             def _():
                 for u in range(2):
-                    i = 2 * s + u
-                    sent[p, 3 * i] = current[u].astype(BF16)
-                    along_a(p, i, 0).start()
-                    along_a(p, i, 1).start()
+                    send_whole(u, 2 * s + u)
 
             @pl.when(side)
             def _():
@@ -298,7 +304,7 @@
 
             return carry
 
-        lax.fori_loop(0, 8, one_step, 0)
+        lax.fori_loop(1, 8, one_step, 0)
 
         sent[p, 14, upper] = summed(p, 1, upper, 2, 5).astype(BF16)
         along_b(p, 5).start()

time: 71.3 us -> 70.5 us (0.989)
  Pallas kernels: 70.6 us -> 69.7 us
    pallas_call x1, Pallas kernels: 69.8 us -> 69 us  [local(): pl.pallas_call(kernel, out_shape=(out, out), in_specs=[pl.BlockSpec(memor...]
where the time goes in v5:
time: 70.5 us; the launch traced here: 70.4 us
  Pallas kernels  69.7 us (99%)
    pallas_call x1, Pallas kernels, local(): pl.pallas_call(kernel, out_shape=(out, out), in_specs=[pl.BlockSpec(memor...  69 us

profile of v5, /device:TPU:1, one launch (start us, length us, event | category | flops | bytes accessed | tf_op | source)
XLA Modules:
  0.0 70.4 jit_solution(11839345045458251316)
XLA Ops:
  0.6 69.0 %propagate_twice.1 = (bf16[384,256]{1,0:T(8,128)(2,1)S(1)}, bf16[384,256]{1,0:T(8,128)(2,1)S(1)}) custom-call(bf16[384,256]{1,0:T(8,128)(2,1)} %cot_hbm.1, s32[3,128]{1,0:T(4,128)} %bitcast.9, s32[16,24]{1,0:T(8,128)} %bitcast.6, s32[16,24]{1,0:T(8,128)} %bitcast.7, s32[16,24]{1,0:T(8,128)} %bitcast.8, bf16[384,128,128]{2,1,0:T(8,128)(2,1)} %bitcast.5), custom_call_target="tpu_custom_call" | custom-call | tf_op jit(solution)/shard_map/propagate_twice/pallas_call | solution.py:360
  69.6 0.8 %finish_results.1 = (bf16[384,256]{1,0:T(8,128)(2,1)}, bf16[384,256]{1,0:T(8,128)(2,1)}) custom-call(bf16[384,256]{1,0:T(8,128)(2,1)S(1)} %get-tuple-element.4.first_in, bf16[384,256]{1,0:T(8,128)(2,1)S(1)} %get-tuple-element.5.label_in), custom_call_target="tpu_custom_call" | custom-call | tf_op jit(solution)/shard_map/finish_results/pallas_call | solution.py:399

commit v6 on v5

--- a/solution.py
+++ b/solution.py
@@ -310,6 +310,14 @@
         along_b(p, 5).start()
         sent[p, 13, lower] = summed(p, 2, lower, 3, 4).astype(BF16)
         along_b(p, 3).start()
+        if p == 1:
+            for q in range(2):
+                for j in range(N_GATHER):
+                    gather_copy(q, j).wait_send()
+            for kind in range(6):
+                for i in range(4):
+                    along_a(0, i, kind).wait_send()
+                along_b(0, kind).wait_send()
         total = summed(p, 1, lower, 3, 4)
         along_b(p, 1).wait_recv()
         sent[p, 14, lower] = (total + got[p, 12, lower].astype(F32)).astype(BF16)
@@ -320,6 +328,10 @@
         along_b(p, 2).start()
         own[3, upper] = summed(p, 3, upper, 2, 5)
         own[3, lower] = summed(p, 3, lower, 3, 4)
+        if p == 1:
+            for kind in range(6):
+                for i in range(4):
+                    along_a(1, i, kind).wait_send()
         for top, from_left, from_right in ((0, 2, 5), (half, 3, 4)):
             rows = pl.ds(top, half)
             along_b(p, from_left).wait_recv()
@@ -338,13 +350,8 @@
                     total + (1.0 - ALPHA) * keep[rows] * (cot_ref[rows].astype(F32) + first_ref[rows].astype(F32))
                 ).astype(BF16)
 
-    for p in range(2):
-        for j in range(N_GATHER):
-            gather_copy(p, j).wait_send()
-        for kind in range(6):
-            for i in range(4):
-                along_a(p, i, kind).wait_send()
-            along_b(p, kind).wait_send()
+    for kind in range(6):
+        along_b(1, kind).wait_send()
 
 
 def hand_over(first_in, label_in, first_out, label_out):

time: 70.5 us -> 70.4 us (level)
  no operation moved by 1% of the time
where the time goes in v6:
time: 70.4 us; the launch traced here: 70.3 us
  Pallas kernels  69.6 us (99%)
    pallas_call x1, Pallas kernels, local(): pl.pallas_call(kernel, out_shape=(out, out), in_specs=[pl.BlockSpec(memor...  68.9 us

profile of v6, /device:TPU:1, one launch (start us, length us, event | category | flops | bytes accessed | tf_op | source)
XLA Modules:
  0.0 70.3 jit_solution(17438411571512437100)
XLA Ops:
  0.6 68.9 %propagate_twice.1 = (bf16[384,256]{1,0:T(8,128)(2,1)S(1)}, bf16[384,256]{1,0:T(8,128)(2,1)S(1)}) custom-call(bf16[384,256]{1,0:T(8,128)(2,1)} %cot_hbm.1, s32[3,128]{1,0:T(4,128)} %bitcast.9, s32[16,24]{1,0:T(8,128)} %bitcast.6, s32[16,24]{1,0:T(8,128)} %bitcast.7, s32[16,24]{1,0:T(8,128)} %bitcast.8, bf16[384,128,128]{2,1,0:T(8,128)(2,1)} %bitcast.5), custom_call_target="tpu_custom_call" | custom-call | tf_op jit(solution)/shard_map/propagate_twice/pallas_call | solution.py:367
  69.5 0.8 %finish_results.1 = (bf16[384,256]{1,0:T(8,128)(2,1)}, bf16[384,256]{1,0:T(8,128)(2,1)}) custom-call(bf16[384,256]{1,0:T(8,128)(2,1)S(1)} %get-tuple-element.4.first_in, bf16[384,256]{1,0:T(8,128)(2,1)S(1)} %get-tuple-element.5.label_in), custom_call_target="tpu_custom_call" | custom-call | tf_op jit(solution)/shard_map/finish_results/pallas_call | solution.py:406

commit v7 on v6

--- a/solution.py
+++ b/solution.py
@@ -93,19 +93,6 @@
 
     small[0].wait()
     small[1].wait()
-    for block in range(segment // tile):
-        seeds = jnp.broadcast_to(seed_ref[block : block + 1, :], (tile, tile)).T
-        lanes = lax.broadcasted_iota(jnp.int32, (tile, tile), 1)
-        rows = slice(block * tile, (block + 1) * tile)
-        for c in range(classes // tile):
-            lane = slice(c * tile, (c + 1) * tile)
-            kept = jnp.where(seeds == lanes + c * tile, 0.0, 1.0)
-            keep[rows, lane] = kept
-            masked = (cot_ref[rows, lane].astype(F32) * kept).astype(BF16)
-            for part in range(tile // sub):
-                gathered0[col * per + block * (tile // sub) + part, :, lane] = masked[part * sub : (part + 1) * sub]
-
-    pl.semaphore_wait(barrier, 7)
 
     def gather_copy(p, j):
         seg_left = ((z + 3) % RING) * 2 + core
@@ -178,10 +165,6 @@
     def along_b(p, kind):
         return reduce_copy(p, 4, kind, b_right, b_left)
 
-    def start_gather(p):
-        for j in (0, 2, 6, 1, 3):
-            gather_copy(p, j).start()
-
     def finish_gather(p):
         arrival(p, 0).wait_recv()
         gather_copy(p, 4).start()
@@ -200,7 +183,22 @@
         for j in range(6, N_GATHER):
             arrival(p, j).wait_recv()
 
-    start_gather(0)
+    for block in range(segment // tile):
+        seeds = jnp.broadcast_to(seed_ref[block : block + 1, :], (tile, tile)).T
+        lanes = lax.broadcasted_iota(jnp.int32, (tile, tile), 1)
+        rows = slice(block * tile, (block + 1) * tile)
+        for c in range(classes // tile):
+            lane = slice(c * tile, (c + 1) * tile)
+            kept = jnp.where(seeds == lanes + c * tile, 0.0, 1.0)
+            keep[rows, lane] = kept
+            masked = (cot_ref[rows, lane].astype(F32) * kept).astype(BF16)
+            for part in range(tile // sub):
+                gathered0[col * per + block * (tile // sub) + part, :, lane] = masked[part * sub : (part + 1) * sub]
+        if block == 1:
+            pl.semaphore_wait(barrier, 7)
+            gather_copy(0, 0).start()
+    for j in (2, 6, 1, 3):
+        gather_copy(0, j).start()
 
     for load in small[2:]:
         load.wait()

time: 70.4 us -> 70.5 us (level)
  no operation moved by 1% of the time
where the time goes in v7:
time: 70.5 us; the launch traced here: 70.4 us
  Pallas kernels  69.7 us (99%)
    pallas_call x1, Pallas kernels, local(): pl.pallas_call(kernel, out_shape=(out, out), in_specs=[pl.BlockSpec(memor...  69 us

profile of v7, /device:TPU:1, one launch (start us, length us, event | category | flops | bytes accessed | tf_op | source)
XLA Modules:
  0.0 70.4 jit_solution(621249254051625444)
XLA Ops:
  0.6 69.0 %propagate_twice.1 = (bf16[384,256]{1,0:T(8,128)(2,1)S(1)}, bf16[384,256]{1,0:T(8,128)(2,1)S(1)}) custom-call(bf16[384,256]{1,0:T(8,128)(2,1)} %cot_hbm.1, s32[3,128]{1,0:T(4,128)} %bitcast.9, s32[16,24]{1,0:T(8,128)} %bitcast.6, s32[16,24]{1,0:T(8,128)} %bitcast.7, s32[16,24]{1,0:T(8,128)} %bitcast.8, bf16[384,128,128]{2,1,0:T(8,128)(2,1)} %bitcast.5), custom_call_target="tpu_custom_call" | custom-call | tf_op jit(solution)/shard_map/propagate_twice/pallas_call | solution.py:365
  69.6 0.8 %finish_results.1 = (bf16[384,256]{1,0:T(8,128)(2,1)}, bf16[384,256]{1,0:T(8,128)(2,1)}) custom-call(bf16[384,256]{1,0:T(8,128)(2,1)S(1)} %get-tuple-element.4.first_in, bf16[384,256]{1,0:T(8,128)(2,1)S(1)} %get-tuple-element.5.label_in), custom_call_target="tpu_custom_call" | custom-call | tf_op jit(solution)/shard_map/finish_results/pallas_call | solution.py:404
